TPU v7x, 32 devices: a whole 2x2x4 slice. The times are simulated.
32 devices in a mesh: shard: 4 (over z), tensor: 4 (over x, core), section: 2 (over y).
Axes of the slice: x: 2, y: 2, z: 4, core: 2. Of those that a mesh axis runs over, the one named last changes fastest.
Arguments:
- hidden_acts: bfloat16 [2, 10240, 4096], P('section', 'shard', 'tensor'), may hold values from -8 to 8
- out_grads: bfloat16 [2, 10240, 1024], P('section', 'shard'), may hold values from -8 to 8
- errors: float32 [2, 4, 1024, 4096], P('section', 'shard', None, 'tensor'), may hold values from -3 to 3
- factors: float32 [2, 32, 4096], P('section', None, 'tensor'), may hold values from -6 to 6
- whiten: float32 [2, 2, 32, 32], P('section'), may hold values from -1.5 to 3
- momentum: float32 [2, 1024, 4096], P('section', 'shard', 'tensor'), may hold values from -3 to 3
- master: float32 [2, 1024, 4096], P('section', 'shard', 'tensor'), may hold values from -3 to 3
- table: bfloat16 [32768, 1024], P(('shard', 'section'), 'tensor'), may hold values from -5 to 5
- touched_ids: int32 [1024], P(('shard', 'section')), may hold values from 0 to 32767, as said below
- touched_grads: bfloat16 [1024, 1024], P(('shard', 'section'), 'tensor'), may hold values from -5 to 5
Outputs:
- new_errors: float32 [2, 4, 1024, 4096], P('section', 'shard', None, 'tensor')
- new_factors: float32 [2, 32, 4096], P('section', None, 'tensor')
- new_momentum: float32 [2, 1024, 4096], P('section', 'shard', 'tensor')
- new_master: float32 [2, 1024, 4096], P('section', 'shard', 'tensor')
- new_weights: bfloat16 [2, 1024, 4096], P('section', None, 'tensor')
- new_table: bfloat16 [32768, 1024], P(('shard', 'section'), 'tensor')
Inputs may be any that keep to these rules, and one draw needn't show every extreme that they name: `touched_ids`: the 128 ids of one device of shard and section name at most 32 rows in each block of 4096 vocabulary rows; in every draw one block receives exactly 32 rows from every device.
All inputs are finite; a program needn't handle non-finite values.
Results may differ from a plain program's by a relative error of at most 0.0036.
Values may be sent and summed in bfloat16 or wider, within the bound.
A program may use at most 128 MiB of HBM per device.

v0:
```python
import jax
import jax.numpy as jnp
from jax import lax
from jax.sharding import PartitionSpec as P

D = 1024
FF = 4096
ROUNDS = 2
epsilon = 1e-06
momentum_decay = 0.9
learn_rate = 0.1
embed_rate = 0.25
clip_level = 0.03
highest = lax.Precision.HIGHEST


def on_device(
    hidden_acts,
    out_grads,
    errors,
    factors,
    whiten,
    momentum,
    master,
    table,
    touched_ids,
    touched_grads,
):
    shards = lax.axis_size("shard")
    grad_block = lax.dot_general(
        out_grads[0], hidden_acts[0], (((0,), (0,)), ((), ())), preferred_element_type=jnp.float32
    )
    rounded = lax.optimization_barrier(grad_block.astype(jnp.bfloat16))
    corrected = rounded.astype(jnp.float32) + errors[0, 0]
    right_part = factors[0]
    rank_count = right_part.shape[0]
    left_unit = None
    for power_round in range(ROUNDS):
        left_part = lax.dot_general(
            right_part,
            corrected,
            (((1,), (1,)), ((), ())),
            precision=highest,
            preferred_element_type=jnp.float32,
        )
        left_sum = lax.psum(left_part, ("shard", "tensor"))
        whitened = jnp.dot(whiten[0, power_round].T, left_sum, precision=highest)
        scaling = lax.rsqrt(jnp.sum(whitened * whitened) / rank_count + epsilon)
        left_unit = whitened * scaling
        right_local = jnp.dot(left_unit, corrected, precision=highest)
        right_part = lax.psum(right_local, "shard") / shards
    gram_left = jnp.dot(left_unit, left_unit.T, precision=highest)
    gram_right = jnp.dot(right_part, right_part.T, precision=highest)
    total_squares = lax.psum(jnp.sum(gram_left * gram_right), ("tensor", "section"))
    approx = lax.dot_general(
        left_unit,
        right_part,
        (((0,), (0,)), ((), ())),
        precision=highest,
        preferred_element_type=jnp.float32,
    )
    new_errors = (corrected - approx)[None, None]
    entries = lax.axis_size("section") * D * FF
    spread = jnp.sqrt(total_squares / entries + epsilon)
    clip_factor = jnp.minimum(1.0, clip_level / spread)
    rows_own = momentum.shape[1]
    row_start = lax.axis_index("shard") * rows_own
    approx_rows = lax.dynamic_slice_in_dim(approx, row_start, rows_own, 0)
    new_momentum = momentum_decay * momentum + clip_factor * approx_rows[None]
    new_master = master - learn_rate * new_momentum
    new_weights = lax.all_gather(new_master.astype(jnp.bfloat16), "shard", axis=1, tiled=True)
    new_factors = right_part[None]
    vocab_rows = table.shape[0]
    table_width = table.shape[1]
    first_row = lax.axis_index(("shard", "section")) * vocab_rows
    recv_rows, recv_ids = (
        lax.all_gather(touched_grads, ("shard", "section"), axis=0, tiled=True),
        lax.all_gather(touched_ids, ("shard", "section"), axis=0, tiled=True),
    )
    local_index = recv_ids - first_row
    inside = (local_index >= 0) & (local_index < vocab_rows)
    target = jnp.where(inside, local_index, vocab_rows)
    table_grad = (
        jnp.zeros((vocab_rows, table_width), jnp.float32)
        .at[target]
        .add(recv_rows.astype(jnp.float32), mode="drop")
    )
    new_table = (table.astype(jnp.float32) - embed_rate * table_grad).astype(jnp.bfloat16)
    return (new_errors, new_factors, new_momentum, new_master, new_weights, new_table)


def solution(mesh):
    in_specs = (
        P("section", "shard", "tensor"),
        P("section", "shard", None),
        P("section", "shard", None, "tensor"),
        P("section", None, "tensor"),
        P("section", None, None, None),
        P("section", "shard", "tensor"),
        P("section", "shard", "tensor"),
        P(("shard", "section"), "tensor"),
        P(("shard", "section")),
        P(("shard", "section"), "tensor"),
    )
    out_specs = (
        P("section", "shard", None, "tensor"),
        P("section", None, "tensor"),
        P("section", "shard", "tensor"),
        P("section", "shard", "tensor"),
        P("section", None, "tensor"),
        P(("shard", "section"), "tensor"),
    )
    return jax.shard_map(
        on_device, mesh=mesh, in_specs=in_specs, out_specs=out_specs, check_vma=False
    )
```

profile of v0, /device:TPU:0, one launch (start us, length us, event | category | flops | bytes accessed | tf_op | source)
XLA Modules:
  0.0 398.0 jit_solution(17824651592674097183)
XLA Ops:
  7.2 0.0 all-reduce.5.cloned.1.call-start
  7.2 9.3 %fusion.5 = bf16[1024,1024]{1,0:T(8,128)(2,1)S(1)} fusion(bf16[1,2560,1024]{2,1,0:T(8,128)(2,1)} %param.10, bf16[1,2560,1024]{2,1,0:T(8,128)(2,1)} %param.11), kind=kOutput, calls=%fused_computation.9 | convolution fusion | flops 5369757696 | bytes 12582912 | tf_op jit(solution)/shard_map/dot_general | solution.py:30
  16.6 4.7 %convolution_bitcast_fusion = f32[32,1024]{1,0:T(8,128)} fusion(f32[1,32,1024]{2,1,0:T(8,128)S(1)} %copy-done, f32[1,1,1024,1024]{3,2,1,0:T(8,128)S(1)} %copy-done.1, bf16[1024,1024]{1,0:T(8,128)(2,1)S(1)} %fusion.5), kind=kOutput, calls=%fused_computation.10 | convolution fusion | flops 404750336 | bytes 6553600 | tf_op jit(solution)/shard_map/dot_general | solution.py:39
  21.2 0.0 all-reduce.5.cloned.1.call-update
  21.3 0.0 all-reduce.7.cloned.1.call-start
  21.3 89.8 %all-reduce.5.cloned.1.call-done = f32[32,1024]{1,0:T(8,128)} async-done(((f32[32,1024]{1,0:T(8,128)}), f32[32,1024]{1,0:T(8,128)}) %all-reduce.5.cloned.1.call-update) | async-done | bytes 131088 | tf_op jit(solution)/shard_map/psum | solution.py:46
  111.1 1.8 multiply_reduce_fusion.1
  113.7 5.6 %fusion.15 = f32[32,1024]{1,0:T(8,128)} fusion(f32[1024,32]{0,1:T(8,128)S(1)} %get-tuple-element.10, f32[]{:T(128)S(6)} %rsqrt.7, f32[1,1,1024,1024]{3,2,1,0:T(8,128)} %param.12, bf16[1024,1024]{1,0:T(8,128)(2,1)S(1)} %fusion.5), kind=kOutput, calls=%fused_computation.20 | convolution fusion | flops 404783104 | bytes 6553604 | tf_op jit(solution)/shard_map/dot_general | solution.py:50
  119.2 0.0 all-reduce.7.cloned.1.call-update
  119.2 0.0 all-reduce.9.cloned.1.call-start
  119.3 36.2 %all-reduce.7.cloned.1.call-done = f32[32,1024]{1,0:T(8,128)} async-done(((f32[32,1024]{1,0:T(8,128)}), f32[32,1024]{1,0:T(8,128)}) %all-reduce.7.cloned.1.call-update) | async-done | bytes 131088 | tf_op jit(solution)/shard_map/psum | solution.py:51
  155.5 6.8 %fusion.13 = f32[32,1024]{1,0:T(8,128)} fusion(f32[32,1024]{1,0:T(8,128)} %all-reduce.7.cloned.1.call-done, f32[1,1,1024,1024]{3,2,1,0:T(8,128)} %param.12, bf16[1024,1024]{1,0:T(8,128)(2,1)S(1)} %fusion.5), kind=kOutput, calls=%fused_computation.18 | convolution fusion | flops 404783104 | bytes 6553600 | tf_op jit(solution)/shard_map/dot_general | solution.py:39
  162.3 0.2 all-reduce.11.cloned.1.call-start
  162.5 86.6 %all-reduce.9.cloned.1.call-done = f32[32,1024]{1,0:T(8,128)} async-done(((f32[32,1024]{1,0:T(8,128)}), f32[32,1024]{1,0:T(8,128)}) %all-reduce.9.cloned.1.call-update) | async-done | bytes 131088 | tf_op jit(solution)/shard_map/psum | solution.py:46
  249.1 1.8 multiply_reduce_fusion
  251.6 5.6 %fusion.23 = f32[32,1024]{1,0:T(8,128)} fusion(f32[1024,32]{0,1:T(8,128)S(1)} %get-tuple-element.12, f32[]{:T(128)S(6)} %rsqrt.8, f32[1,1,1024,1024]{3,2,1,0:T(8,128)} %param.12, bf16[1024,1024]{1,0:T(8,128)(2,1)S(1)} %fusion.5), kind=kOutput, calls=%fused_computation.30 | convolution fusion | flops 404783104 | bytes 6553604 | tf_op jit(solution)/shard_map/dot_general | solution.py:50
  257.3 0.0 all-gather.3.cloned.1.call-start
  257.3 0.2 fusion.20
  257.6 36.0 %all-reduce.11.cloned.1.call-done = f32[32,1024]{1,0:T(8,128)} async-done(((f32[32,1024]{1,0:T(8,128)}), f32[32,1024]{1,0:T(8,128)}) %all-reduce.11.cloned.1.call-update) | async-done | bytes 131088 | tf_op jit(solution)/shard_map/psum | solution.py:51
  293.6 1.8 fusion.11
  295.4 14.0 %psum.39 = f32[]{:T(128)} all-reduce(f32[]{:T(128)} %fusion.11), channel_id=1, replica_groups=mesh['shard'=4,'tensor'=4,'section'=2] {'tensor','section'}, use_global_device_ids=true, to_apply=%region_7.0 | all-reduce | flops 1 | bytes 8 | tf_op jit(solution)/shard_map/psum | solution.py:54
  310.1 4.5 %fusion.18 = f32[1024,1024]{1,0:T(8,128)S(1)} fusion(f32[32,1024]{1,0:T(8,128)} %all-reduce.11.cloned.1.call-done, f32[1024,32]{0,1:T(8,128)S(1)} %get-tuple-element.12, f32[]{:T(128)S(6)} %rsqrt.8), kind=kOutput, calls=%fused_computation.25 | convolution fusion | flops 402718720 | bytes 4456452 | tf_op jit(solution)/shard_map/dot_general | solution.py:55
  314.6 2.0 copy-done.3
  316.6 1.9 fusion.41
  318.6 18.6 %all-gather = s32[8,1,128]{2,1,0:T(1,128)S(1)} all-gather(s32[1,1,128]{2,1,0:T(1,128)S(1)} %bitcast.48), channel_id=1, replica_groups=mesh['shard'=4,'tensor'=4,'section'=2] {'shard','section'}, dimensions={0}, use_global_device_ids=true | all-gather | bytes 4608 | tf_op jit(solution)/shard_map/all_gather | solution.py:78
  337.2 33.2 %all_gather.11 = bf16[1024,256]{1,0:T(8,128)(2,1)S(1)} all-gather(bf16[128,256]{1,0:T(8,128)(2,1)S(1)} %copy-done.8), channel_id=1, replica_groups=mesh['shard'=4,'tensor'=4,'section'=2] {'shard','section'}, dimensions={0}, use_global_device_ids=true | all-gather | bytes 589824 | tf_op jit(solution)/shard_map/all_gather | solution.py:77
  370.3 8.3 %scatter_custom_fusion = f32[4096,256]{1,0:T(8,128)} fusion(s32[1024]{0:T(1024)S(1)} %compare_select_fusion, f32[]{:T(128)} %constant.16.clone.1, bf16[1024,256]{1,0:T(8,128)(2,1)S(1)} %all_gather.11), kind=kCustom, calls=%fused_computation.7 | custom fusion | flops 524288 | bytes 4718596 | tf_op jit(solution)/shard_map/scatter-add | solution.py:86
  378.6 4.8 %subtract_convert_fusion = bf16[4096,256]{1,0:T(8,128)(2,1)} fusion(f32[4096,256]{1,0:T(8,128)} %scatter_custom_fusion, bf16[4096,256]{1,0:T(8,128)(2,1)} %param.17), kind=kLoop, calls=%fused_computation.5 | loop fusion | flops 4194304 | bytes 8388608 | tf_op jit(solution)/shard_map/convert_element_type | solution.py:88
  383.4 0.7 multiply_bitcast_fusion
  384.1 0.6 copy-done.4
  384.7 3.6 subtract_bitcast_fusion
  388.3 3.1 copy.21
  (26 shorter events, 0.1 us)
Async XLA Ops:
  7.2 9.4 %copy-start = (f32[1,32,1024]{2,1,0:T(8,128)S(1)}, f32[1,32,1024]{2,1,0:T(8,128)}, u32[]{:S(2)}) copy-start(f32[1,32,1024]{2,1,0:T(8,128)} %param.13) | copy-start | bytes 393220
  7.2 103.9 %all-reduce.5.cloned.1.call-start = ((), (), s32[]{:S(2)}) async-start(), calls=%async_computation | async-start | bytes 262144 | tf_op jit(solution)/shard_map/psum | solution.py:46
  7.2 9.3 %copy-start.1 = (f32[1,1,1024,1024]{3,2,1,0:T(8,128)S(1)}, f32[1,1,1024,1024]{3,2,1,0:T(8,128)}, u32[]{:S(2)}) copy-start(f32[1,1,1024,1024]{3,2,1,0:T(8,128)} %param.12) | copy-start | bytes 12582916
  16.5 94.6 %copy-start.9 = (f32[1,2,32,32]{3,2,1,0:T(8,128)S(1)}, f32[1,2,32,32]{3,2,1,0:T(8,128)}, u32[]{:S(2)}) copy-start(f32[1,2,32,32]{3,2,1,0:T(8,128)} %param.14) | copy-start | bytes 24580
  21.3 134.2 %all-reduce.7.cloned.1.call-start = ((), (), s32[]{:S(2)}) async-start(), calls=%async_computation.1 | async-start | bytes 262144 | tf_op jit(solution)/shard_map/psum | solution.py:51
  119.2 129.8 %all-reduce.9.cloned.1.call-start = ((), (), s32[]{:S(2)}) async-start(), calls=%async_computation.2 | async-start | bytes 262144 | tf_op jit(solution)/shard_map/psum | solution.py:46
  162.3 131.3 %all-reduce.11.cloned.1.call-start = ((), (), s32[]{:S(2)}) async-start(), calls=%async_computation.3 | async-start | bytes 262144 | tf_op jit(solution)/shard_map/psum | solution.py:51
  251.6 65.0 %copy-start.6 = (f32[1,256,1024]{2,1,0:T(8,128)S(1)}, f32[1,256,1024]{2,1,0:T(8,128)}, u32[]{:S(2)}) copy-start(f32[1,256,1024]{2,1,0:T(8,128)} %param.16) | copy-start | bytes 3145732
  257.3 131.1 %all-gather.3.cloned.1.call-start = ((), (), s32[]{:S(2)}) async-start(), calls=%async_computation.4 | async-start | bytes 2621440 | tf_op jit(solution)/shard_map/all_gather | solution.py:71
  310.1 6.5 %copy-start.7 = (f32[1,256,1024]{2,1,0:T(8,128)S(1)}, f32[1,256,1024]{2,1,0:T(8,128)}, u32[]{:S(2)}) copy-start(f32[1,256,1024]{2,1,0:T(8,128)} %param.15) | copy-start | bytes 3145732
  314.6 2.0 copy-start.3
  316.6 2.0 copy-start.10
  316.6 20.6 %copy-start.8 = (bf16[128,256]{1,0:T(8,128)(2,1)S(1)}, bf16[128,256]{1,0:T(8,128)(2,1)}, u32[]{:S(2)}) copy-start(bf16[128,256]{1,0:T(8,128)(2,1)} %param.19) | copy-start | bytes 196612
  370.3 13.1 %copy-start.5 = (f32[32,1024]{1,0:T(8,128)S(1)}, f32[32,1024]{1,0:T(8,128)}, u32[]{:S(2)}) copy-start(f32[32,1024]{1,0:T(8,128)} %all-reduce.11.cloned.1.call-done) | copy-start | bytes 393220
  378.6 5.5 %copy-start.2 = (f32[1,1,1024,1024]{3,2,1,0:T(8,128)S(1)}, f32[1,1,1024,1024]{3,2,1,0:T(8,128)}, u32[]{:S(2)}) copy-start(f32[1,1,1024,1024]{3,2,1,0:T(8,128)} %param.12) | copy-start | bytes 12582916
  378.6 6.1 %copy-start.4 = (f32[1024,1024]{1,0:T(8,128)S(1)}, f32[1024,1024]{1,0:T(8,128)}, u32[]{:S(2)}) copy-start(f32[1024,1024]{1,0:T(8,128)} %copy-done.3) | copy-start | bytes 12582916
Sparse Core Ops, SparseCore 0:
  21.4 89.6 all-reduce.4
  119.4 36.0 all-reduce.6
  162.4 86.6 all-reduce.8
  257.4 36.1 all-reduce.10
  318.7 49.5 all-gather.2
where the time goes:
time: 398 us
  waiting for transfers between devices  249 us (63%)
  blocking collectives  65.7 us (17%)
  matrix products  42.2 us (11%)
  other arithmetic  19.3 us (5%)
  between operations  16 us (4%)
  local copies, waits for them, and re-layouts  5.77 us (1%)
    psum x2, waiting for transfers between devices, on_device(): left_sum = lax.psum(left_part, ('shard', 'tensor'))  176 us
    psum x2, waiting for transfers between devices, on_device(): right_part = lax.psum(right_local, 'shard') / shards  72.2 us
    all_gather x1, blocking collectives, on_device(): lax.all_gather(touched_grads, ('shard', 'section'), axis=0, tiled=True)  33.2 us
    all_gather x1, blocking collectives, on_device(): lax.all_gather(touched_ids, ('shard', 'section'), axis=0, tiled=True)  18.6 us
    psum x1, blocking collectives, on_device(): lax.psum(jnp.sum(gram_left * gram_right), ('tensor', 'section'))  14 us
    dot_general x2, matrix products, on_device(): lax.dot_general(right_part, corrected, (((1,), (1,)), ((), ())), precisio...  11.4 us
    dot_general x2, matrix products, on_device(): right_local = jnp.dot(left_unit, corrected, precision=highest)  11.2 us
    dot_general x1, matrix products, on_device(): lax.dot_general(out_grads[0], hidden_acts[0], (((0,), (0,)), ((), ())), p...  9.28 us
  transfers between devices with their start and end apart: 5, of which 4 were waited for; matrix products, arithmetic and copies ran while one was open for 4% of the time, Pallas kernels for 0%

commit v1 on v0

--- a/solution.py
+++ b/solution.py
@@ -48,7 +48,7 @@
         scaling = lax.rsqrt(jnp.sum(whitened * whitened) / rank_count + epsilon)
         left_unit = whitened * scaling
         right_local = jnp.dot(left_unit, corrected, precision=highest)
-        right_part = lax.psum(right_local, "shard") / shards
+        right_part = jnp.sum(lax.all_gather(right_local, "shard"), axis=0) / shards
     gram_left = jnp.dot(left_unit, left_unit.T, precision=highest)
     gram_right = jnp.dot(right_part, right_part.T, precision=highest)
     total_squares = lax.psum(jnp.sum(gram_left * gram_right), ("tensor", "section"))

time: 398 us -> 360 us (0.905)
  waiting for transfers between devices: 249 us -> 177 us
  blocking collectives: 65.7 us -> 101 us
    psum x2 -> x0, waiting for transfers between devices: 72.2 us -> none  [on_device(): right_part = lax.psum(right_local, 'shard') / shards]
    all_gather x0 -> x2, blocking collectives: none -> 34.5 us  [on_device(): right_part = jnp.sum(lax.all_gather(right_local, 'shard'), axis=0) / shards]
  transfers between devices with their start and end apart: 5 -> 3, of which waited for: 4 -> 2; matrix products, arithmetic and copies ran while one was open for 4% -> 5% of each run, Pallas kernels for 0% -> 0%
where the time goes in v1:
time: 360 us; the launch traced here: 359 us
  waiting for transfers between devices  177 us (49%)
  blocking collectives  101 us (28%)
  matrix products  40.3 us (11%)
  other arithmetic  21.4 us (6%)
  between operations  15.9 us (4%)
  local copies, waits for them, and re-layouts  3.75 us (1%)
    psum x2, waiting for transfers between devices, on_device(): left_sum = lax.psum(left_part, ('shard', 'tensor'))  177 us
    all_gather x2, blocking collectives, on_device(): right_part = jnp.sum(lax.all_gather(right_local, 'shard'), axis=0) / shards  34.5 us
    all_gather x1, blocking collectives, on_device(): lax.all_gather(touched_grads, ('shard', 'section'), axis=0, tiled=True)  33.1 us
    all_gather x1, blocking collectives, on_device(): lax.all_gather(touched_ids, ('shard', 'section'), axis=0, tiled=True)  19.5 us
    psum x1, blocking collectives, on_device(): lax.psum(jnp.sum(gram_left * gram_right), ('tensor', 'section'))  14 us
    dot_general x2, matrix products, on_device(): lax.dot_general(right_part, corrected, (((1,), (1,)), ((), ())), precisio...  11.4 us
    dot_general x2, matrix products, on_device(): right_local = jnp.dot(left_unit, corrected, precision=highest)  9.81 us
    dot_general x1, matrix products, on_device(): lax.dot_general(out_grads[0], hidden_acts[0], (((0,), (0,)), ((), ())), p...  9.28 us
  transfers between devices with their start and end apart: 3, of which 2 were waited for; matrix products, arithmetic and copies ran while one was open for 5% of the time, Pallas kernels for 0%

profile of v1, /device:TPU:0, one launch (start us, length us, event | category | flops | bytes accessed | tf_op | source)
XLA Modules:
  0.0 359.5 jit_solution(8757713297570547361)
XLA Ops:
  7.2 0.0 copy-start
  7.2 0.0 all-reduce.3.cloned.1.call-start
  7.2 9.3 %fusion.5 = bf16[1024,1024]{1,0:T(8,128)(2,1)S(1)} fusion(bf16[1,2560,1024]{2,1,0:T(8,128)(2,1)} %param.10, bf16[1,2560,1024]{2,1,0:T(8,128)(2,1)} %param.11), kind=kOutput, calls=%fused_computation.9 | convolution fusion | flops 5369757696 | bytes 12582912 | tf_op jit(solution)/shard_map/dot_general | solution.py:30
  16.5 0.0 copy-start.5
  16.6 4.7 %convolution_bitcast_fusion = f32[32,1024]{1,0:T(8,128)} fusion(f32[1,32,1024]{2,1,0:T(8,128)S(1)} %copy-done, f32[1,1,1024,1024]{3,2,1,0:T(8,128)S(1)} %copy-done.1, bf16[1024,1024]{1,0:T(8,128)(2,1)S(1)} %fusion.5), kind=kOutput, calls=%fused_computation.10 | convolution fusion | flops 404750336 | bytes 6553600 | tf_op jit(solution)/shard_map/dot_general | solution.py:39
  21.2 0.0 all-reduce.3.cloned.1.call-update
  21.3 0.0 all-reduce.5.cloned.1.call-start
  21.3 89.9 %all-reduce.3.cloned.1.call-done = f32[32,1024]{1,0:T(8,128)} async-done(((f32[32,1024]{1,0:T(8,128)}), f32[32,1024]{1,0:T(8,128)}) %all-reduce.3.cloned.1.call-update) | async-done | bytes 131088 | tf_op jit(solution)/shard_map/psum | solution.py:46
  111.2 1.8 multiply_reduce_fusion.1
  113.7 4.9 %fusion.15 = f32[32,1024]{1,0:T(8,128)S(1)} fusion(f32[1024,32]{0,1:T(8,128)S(1)} %get-tuple-element.10, f32[]{:T(128)S(6)} %rsqrt.7, f32[1,1,1024,1024]{3,2,1,0:T(8,128)} %param.12, bf16[1024,1024]{1,0:T(8,128)(2,1)S(1)} %fusion.5), kind=kOutput, calls=%fused_computation.20 | convolution fusion | flops 404783104 | bytes 6553604 | tf_op jit(solution)/shard_map/dot_general | solution.py:50
  118.7 17.3 %all-gather = f32[128,1024]{1,0:T(8,128)S(1)} all-gather(f32[32,1024]{1,0:T(8,128)S(1)} %fusion.15), channel_id=2, replica_groups=mesh['shard'=4,'tensor'=4,'section'=2] {'shard'}, dimensions={0}, use_global_device_ids=true | all-gather | bytes 655360 | tf_op jit(solution)/shard_map/all_gather | solution.py:51
  135.9 6.7 %fusion.13 = f32[32,1024]{1,0:T(8,128)} fusion(f32[32,1024]{1,0:T(8,128)S(1)} %reduce_sum.46, f32[1,1,1024,1024]{3,2,1,0:T(8,128)} %param.12, bf16[1024,1024]{1,0:T(8,128)(2,1)S(1)} %fusion.5), kind=kOutput, calls=%fused_computation.18 | convolution fusion | flops 404783104 | bytes 6553600 | tf_op jit(solution)/shard_map/dot_general | solution.py:39
  142.6 0.0 all-reduce.5.cloned.1.call-update
  142.7 0.2 all-gather.5.cloned.1.call-start
  142.9 86.7 %all-reduce.5.cloned.1.call-done = f32[32,1024]{1,0:T(8,128)} async-done(((f32[32,1024]{1,0:T(8,128)}), f32[32,1024]{1,0:T(8,128)}) %all-reduce.5.cloned.1.call-update) | async-done | bytes 131088 | tf_op jit(solution)/shard_map/psum | solution.py:46
  229.6 1.8 multiply_reduce_fusion
  232.1 0.3 fusion.20
  232.4 4.9 %fusion.23 = f32[32,1024]{1,0:T(8,128)S(1)} fusion(f32[1024,32]{0,1:T(8,128)S(1)} %get-tuple-element.12, f32[]{:T(128)S(6)} %rsqrt.8, f32[1,1,1024,1024]{3,2,1,0:T(8,128)} %param.12, bf16[1024,1024]{1,0:T(8,128)(2,1)S(1)} %fusion.5), kind=kOutput, calls=%fused_computation.30 | convolution fusion | flops 404783104 | bytes 6553604 | tf_op jit(solution)/shard_map/dot_general | solution.py:50
  237.3 17.3 %all-gather.1 = f32[128,1024]{1,0:T(8,128)S(1)} all-gather(f32[32,1024]{1,0:T(8,128)S(1)} %fusion.23), channel_id=3, replica_groups=mesh['shard'=4,'tensor'=4,'section'=2] {'shard'}, dimensions={0}, use_global_device_ids=true | all-gather | bytes 655360 | tf_op jit(solution)/shard_map/all_gather | solution.py:51
  254.6 0.9 fusion.11
  255.5 5.0 %fusion.18 = f32[1024,1024]{1,0:T(8,128)} fusion(f32[32,1024]{1,0:T(8,128)S(1)} %reduce_sum.48, f32[1024,32]{0,1:T(8,128)S(1)} %get-tuple-element.12, f32[]{:T(128)S(6)} %rsqrt.8), kind=kOutput, calls=%fused_computation.25 | convolution fusion | flops 402718720 | bytes 4456452 | tf_op jit(solution)/shard_map/dot_general | solution.py:55
  260.5 14.0 %psum.23 = f32[]{:T(128)} all-reduce(f32[]{:T(128)} %fusion.11), channel_id=1, replica_groups=mesh['shard'=4,'tensor'=4,'section'=2] {'tensor','section'}, use_global_device_ids=true, to_apply=%region_7.0 | all-reduce | flops 1 | bytes 8 | tf_op jit(solution)/shard_map/psum | solution.py:54
  275.2 3.9 %fusion.41 = (bf16[1,256,1024]{2,1,0:T(8,128)(2,1)}, f32[1,256,1024]{2,1,0:T(8,128)}, f32[1,256,1024]{2,1,0:T(8,128)}) fusion(f32[1,256,1024]{2,1,0:T(8,128)} %param.16, f32[1024,1024]{1,0:T(8,128)} %fusion.18, s32[]{:T(128)S(6)} %select_n.10, f32[]{:T(128)S(6)} %min_shard_map.3, f32[1,256,1024]{2,1,0:T(8,128)} %param.15), kind=kLoop, calls=%fused_computation.50 | loop fusion | flops 1572864 | bytes 5767176 | tf_op jit(solution)/shard_map/convert_element_type | solution.py:71
  279.1 0.0 all-gather.5.cloned.1.call-update
  279.2 19.5 %all-gather.2 = s32[8,1,128]{2,1,0:T(1,128)S(1)} all-gather(s32[1,1,128]{2,1,0:T(1,128)S(1)} %bitcast.52), channel_id=1, replica_groups=mesh['shard'=4,'tensor'=4,'section'=2] {'shard','section'}, dimensions={0}, use_global_device_ids=true | all-gather | bytes 4608 | tf_op jit(solution)/shard_map/all_gather | solution.py:78
  298.7 33.1 %all_gather.27 = bf16[1024,256]{1,0:T(8,128)(2,1)S(1)} all-gather(bf16[128,256]{1,0:T(8,128)(2,1)S(1)} %copy-done.4), channel_id=1, replica_groups=mesh['shard'=4,'tensor'=4,'section'=2] {'shard','section'}, dimensions={0}, use_global_device_ids=true | all-gather | bytes 589824 | tf_op jit(solution)/shard_map/all_gather | solution.py:77
  331.9 8.3 %scatter_custom_fusion = f32[4096,256]{1,0:T(8,128)} fusion(s32[1024]{0:T(1024)S(1)} %compare_select_fusion, f32[]{:T(128)} %constant.16.clone.1, bf16[1024,256]{1,0:T(8,128)(2,1)S(1)} %all_gather.27), kind=kCustom, calls=%fused_computation.7 | custom fusion | flops 524288 | bytes 4718596 | tf_op jit(solution)/shard_map/scatter-add | solution.py:86
  340.1 4.8 %subtract_convert_fusion = bf16[4096,256]{1,0:T(8,128)(2,1)} fusion(f32[4096,256]{1,0:T(8,128)} %scatter_custom_fusion, bf16[4096,256]{1,0:T(8,128)(2,1)} %param.17), kind=kLoop, calls=%fused_computation.5 | loop fusion | flops 4194304 | bytes 8388608 | tf_op jit(solution)/shard_map/convert_element_type | solution.py:88
  345.0 0.7 multiply_bitcast_fusion
  345.6 0.6 copy-done.3
  346.3 3.6 %subtract_bitcast_fusion = f32[1,1,1024,1024]{3,2,1,0:T(8,128)} fusion(f32[1024,1024]{1,0:T(8,128)S(1)} %copy-done.3, f32[1,1,1024,1024]{3,2,1,0:T(8,128)S(1)} %copy-done.2, bf16[1024,1024]{1,0:T(8,128)(2,1)S(1)} %fusion.5), kind=kLoop, calls=%fused_computation.6 | loop fusion | flops 3145728 | bytes 14680064 | tf_op jit(solution)/shard_map/broadcast_in_dim | solution.py:62
  349.9 3.1 copy.19
  (16 shorter events, 0.1 us)
Async XLA Ops:
  7.2 9.4 %copy-start = (f32[1,32,1024]{2,1,0:T(8,128)S(1)}, f32[1,32,1024]{2,1,0:T(8,128)}, u32[]{:S(2)}) copy-start(f32[1,32,1024]{2,1,0:T(8,128)} %param.13) | copy-start | bytes 393220
  7.2 104.0 %all-reduce.3.cloned.1.call-start = ((), (), s32[]{:S(2)}) async-start(), calls=%async_computation | async-start | bytes 262144 | tf_op jit(solution)/shard_map/psum | solution.py:46
  7.2 9.3 %copy-start.1 = (f32[1,1,1024,1024]{3,2,1,0:T(8,128)S(1)}, f32[1,1,1024,1024]{3,2,1,0:T(8,128)}, u32[]{:S(2)}) copy-start(f32[1,1,1024,1024]{3,2,1,0:T(8,128)} %param.12) | copy-start | bytes 12582916
  16.5 94.7 %copy-start.5 = (f32[1,2,32,32]{3,2,1,0:T(8,128)S(1)}, f32[1,2,32,32]{3,2,1,0:T(8,128)}, u32[]{:S(2)}) copy-start(f32[1,2,32,32]{3,2,1,0:T(8,128)} %param.14) | copy-start | bytes 24580
  21.3 208.3 %all-reduce.5.cloned.1.call-start = ((), (), s32[]{:S(2)}) async-start(), calls=%async_computation.1 | async-start | bytes 262144 | tf_op jit(solution)/shard_map/psum | solution.py:46
  142.7 207.2 %all-gather.5.cloned.1.call-start = ((), (), s32[]{:S(2)}) async-start(), calls=%async_computation.2 | async-start | bytes 2621440 | tf_op jit(solution)/shard_map/all_gather | solution.py:71
  260.5 18.7 %copy-start.6 = (s32[128]{0:T(128)S(1)}, s32[128]{0:T(128)}, u32[]{:S(2)}) copy-start(s32[128]{0:T(128)} %param.18) | copy-start | bytes 1540
  260.5 38.2 %copy-start.4 = (bf16[128,256]{1,0:T(8,128)(2,1)S(1)}, bf16[128,256]{1,0:T(8,128)(2,1)}, u32[]{:S(2)}) copy-start(bf16[128,256]{1,0:T(8,128)(2,1)} %param.19) | copy-start | bytes 196612
  340.1 5.5 %copy-start.2 = (f32[1,1,1024,1024]{3,2,1,0:T(8,128)S(1)}, f32[1,1,1024,1024]{3,2,1,0:T(8,128)}, u32[]{:S(2)}) copy-start(f32[1,1,1024,1024]{3,2,1,0:T(8,128)} %param.12) | copy-start | bytes 12582916
  340.1 6.1 %copy-start.3 = (f32[1024,1024]{1,0:T(8,128)S(1)}, f32[1024,1024]{1,0:T(8,128)}, u32[]{:S(2)}) copy-start(f32[1024,1024]{1,0:T(8,128)} %fusion.18) | copy-start | bytes 12582916
Sparse Core Ops, SparseCore 0:
  21.4 89.7 all-reduce.2
  142.8 86.7 all-reduce.4
  279.3 49.7 all-gather.4
